TPU v7x, 256 devices: a whole 4x4x8 slice. The times are simulated.
256 devices in a mesh: seq: 64 (over z_hi, y, x), ch: 4 (over z_lo, core).
Axes of the slice: x: 4, y: 4, z: 8 (z_hi: 4, z_lo: 2; z = z_hi * 2 + z_lo), core: 2. Of those that a mesh axis runs over, the one named last changes fastest.
Arguments:
- inputs: float32 [256, 32768], P('ch', 'seq'), may hold values from -6 to 6
- w_in: float32 [3, 256, 256], P(None, 'ch'), may hold values from -0.375 to 0.375
- short_w: float32 [3, 3, 256], P(None, None, 'ch'), may hold values from -3 to 3
- filter_param: float32 [256, 32768], P('ch', 'seq'), may hold values from -6 to 6
- skip: float32 [256], P('ch'), may hold values from -4 to 4
- w_out: float32 [256, 256], P('ch'), may hold values from -0.375 to 0.375
- cotangent: float32 [256, 32768], P('ch', 'seq'), may hold values from -6 to 6
Outputs:
- output: float32 [256, 32768], P('ch', 'seq')
- grad_input: float32 [256, 32768], P('ch', 'seq')
- grad_filter: float32 [256, 32768], P('ch', 'seq')
All inputs are finite; a program needn't handle non-finite values.
Results may differ from a plain program's by a relative error of at most 0.0003.
Values sent between devices are 32-bit elements; how exact they have to be, the bound alone decides.
No kernel may reach another device: no remote copies, remote signals or barrier semaphores. Data moves between devices by JAX's collectives and lax.ppermute only.
A program may use at most 64 MiB of HBM per device.

v0:
```python
import math
import jax
import jax.numpy as jnp
from jax import lax
from jax.sharding import PartitionSpec as P

PRECISE = lax.Precision.HIGHEST


def passed_along(block, axis, distance):
    devices = range(lax.axis_size(axis))
    route = [(i - distance, i) for i in devices if i - distance in devices]
    return lax.ppermute(block, axis, route)


def fourier_tables(order):
    indices = jnp.arange(order, dtype=jnp.int32)
    products = indices[:, None] * indices[None, :] % order
    angles = products.astype(jnp.float32) * (2.0 * math.pi / order)
    return (jnp.cos(angles), jnp.sin(angles))


def to_sorted(spec_real, spec_imag):
    count, channels, length = spec_real.shape
    shards = lax.axis_size("seq")
    stacked = jnp.concatenate([spec_real, spec_imag], 0).reshape(
        2 * count, channels, shards, length // shards
    )
    arrived = lax.all_to_all(stacked, "seq", split_axis=2, concat_axis=2, tiled=True)
    arrived = jnp.transpose(arrived, (0, 1, 3, 2)).reshape(2 * count, channels, length)
    return (arrived[:count], arrived[count:])


def from_sorted(spec_real, spec_imag):
    count, channels, length = spec_real.shape
    shards = lax.axis_size("seq")
    stacked = jnp.concatenate([spec_real, spec_imag], 0).reshape(
        2 * count, channels, length // shards, shards
    )
    stacked = jnp.transpose(stacked, (0, 1, 3, 2))
    arrived = lax.all_to_all(stacked, "seq", split_axis=2, concat_axis=2, tiled=True).reshape(
        2 * count, channels, length
    )
    return (arrived[:count], arrived[count:])


def to_spectrum(signal, tables):
    cos_small, sin_small, cos_big, sin_big = tables
    rows_in, channels, length = signal.shape
    shards = lax.axis_size("seq")
    slab_len = length // shards
    full_len = length * shards
    blocks = lax.all_to_all(
        signal.reshape(rows_in, channels, shards, slab_len),
        "seq",
        split_axis=2,
        concat_axis=2,
        tiled=True,
    )
    part_real = jnp.einsum("ks,ncsm->nckm", cos_small, blocks, precision=PRECISE)
    part_imag = -jnp.einsum("ks,ncsm->nckm", sin_small, blocks, precision=PRECISE)
    count = part_real.shape[0]
    positions = lax.axis_index("seq") * slab_len + jnp.arange(slab_len, dtype=jnp.int32)
    residues = jnp.arange(shards, dtype=jnp.int32)
    angles = (residues[:, None] * positions[None, :] % full_len).astype(jnp.float32) * (
        2.0 * math.pi / full_len
    )
    turn_cos = jnp.cos(angles)
    turn_sin = jnp.sin(angles)
    rot_real = part_real * turn_cos + part_imag * turn_sin
    rot_imag = part_imag * turn_cos - part_real * turn_sin
    stacked = jnp.concatenate([rot_real, rot_imag], 0)
    arrived = lax.all_to_all(stacked, "seq", split_axis=2, concat_axis=2, tiled=True).reshape(
        2 * count, channels, length
    )
    row_real = arrived[:count]
    row_imag = arrived[count:]
    spec_real = jnp.einsum("ncj,jk->nck", row_real, cos_big, precision=PRECISE) + jnp.einsum(
        "ncj,jk->nck", row_imag, sin_big, precision=PRECISE
    )
    spec_imag = jnp.einsum("ncj,jk->nck", row_imag, cos_big, precision=PRECISE) - jnp.einsum(
        "ncj,jk->nck", row_real, sin_big, precision=PRECISE
    )
    spec_real, spec_imag = to_sorted(spec_real, spec_imag)
    return (spec_real, spec_imag)


def from_spectrum(spec_real, spec_imag, tables):
    cos_small, sin_small, cos_big, sin_big = tables
    spec_real, spec_imag = from_sorted(spec_real, spec_imag)
    count, channels, length = spec_real.shape
    shards = lax.axis_size("seq")
    slab_len = length // shards
    full_len = length * shards
    row_real = jnp.einsum("nck,kj->ncj", spec_real, cos_big, precision=PRECISE) - jnp.einsum(
        "nck,kj->ncj", spec_imag, sin_big, precision=PRECISE
    )
    row_imag = jnp.einsum("nck,kj->ncj", spec_imag, cos_big, precision=PRECISE) + jnp.einsum(
        "nck,kj->ncj", spec_real, sin_big, precision=PRECISE
    )
    positions = jnp.arange(length, dtype=jnp.int32)
    angles = (positions * lax.axis_index("seq") % full_len).astype(jnp.float32) * (
        2.0 * math.pi / full_len
    )
    turn_cos = jnp.cos(angles)
    turn_sin = jnp.sin(angles)
    rot_real = row_real * turn_cos - row_imag * turn_sin
    rot_imag = row_imag * turn_cos + row_real * turn_sin
    stacked = jnp.concatenate([rot_real, rot_imag], 0).reshape(
        2 * count, channels, shards, slab_len
    )
    arrived = lax.all_to_all(stacked, "seq", split_axis=2, concat_axis=2, tiled=True)
    arrived_real = arrived[:count]
    arrived_imag = arrived[count:]
    pieces = (
        jnp.einsum("sk,nckm->ncsm", cos_small, arrived_real, precision=PRECISE)
        - jnp.einsum("sk,nckm->ncsm", sin_small, arrived_imag, precision=PRECISE)
    ) / full_len
    restored = lax.all_to_all(pieces, "seq", split_axis=2, concat_axis=2, tiled=True)
    return restored.reshape(pieces.shape[0], channels, length)


def body(inputs, w_in, short_w, filter_param, skip, w_out, cotangent):
    channels, length = inputs.shape
    shards = lax.axis_size("seq")
    filter_scale = (length * shards) ** (-0.5)
    cos_small, sin_small = fourier_tables(shards)
    cos_big, sin_big = fourier_tables(length)
    tables = (cos_small, sin_small, cos_big, sin_big)
    columns = w_in
    projected = jnp.einsum(
        "icd,dt->ict", columns, lax.all_gather(inputs, "ch", axis=0, tiled=True), precision=PRECISE
    )
    tap_first = short_w[0][:, :, None]
    tap_second = short_w[1][:, :, None]
    tap_third = short_w[2][:, :, None]
    before = passed_along(projected[:, :, length - 2 :], "seq", 1)
    widened = jnp.concatenate([before, projected], 2)
    convolved = (
        tap_first * projected
        + tap_second * widened[:, :, 1 : length + 1]
        + tap_third * widened[:, :, 0:length]
    )
    gated = convolved[1] * convolved[2]
    filter_taps = filter_param * filter_scale
    spec_real, spec_imag = to_spectrum(jnp.stack([gated, filter_taps]), tables)
    gated_real, gated_imag = (spec_real[0], spec_imag[0])
    filt_real, filt_imag = (spec_real[1], spec_imag[1])
    prod_real = filt_real * gated_real - filt_imag * gated_imag
    prod_imag = filt_real * gated_imag + filt_imag * gated_real
    convolution = from_spectrum(prod_real[None], prod_imag[None], tables)[0]
    mixed = convolution + skip[:, None] * gated
    out_gate = convolved[0] * mixed
    columns = w_out
    output = jnp.dot(columns, lax.all_gather(out_gate, "ch", axis=0, tiled=True), precision=PRECISE)
    columns = w_out
    grad_gate = lax.psum_scatter(
        jnp.dot(columns.T, cotangent, precision=PRECISE), "ch", scatter_dimension=0, tiled=True
    )
    grad_mixed = convolved[0] * grad_gate
    grad_first = mixed * grad_gate
    grad_spec_real, grad_spec_imag = to_spectrum(grad_mixed[None], tables)
    grad_real = grad_spec_real[0]
    grad_imag = grad_spec_imag[0]
    corr_real = filt_real * grad_real + filt_imag * grad_imag
    corr_imag = filt_real * grad_imag - filt_imag * grad_real
    taps_real = grad_real * gated_real + grad_imag * gated_imag
    taps_imag = grad_imag * gated_real - grad_real * gated_imag
    restored = from_spectrum(
        jnp.stack([corr_real, taps_real]), jnp.stack([corr_imag, taps_imag]), tables
    )
    grad_gated = restored[0] + skip[:, None] * grad_mixed
    grad_filter = restored[1] * filter_scale
    grad_conv = jnp.stack([grad_first, grad_gated * convolved[2], grad_gated * convolved[1]])
    beyond = passed_along(grad_conv[:, :, 0:2], "seq", -1)
    extended = jnp.concatenate([grad_conv, beyond], 2)
    grad_proj = (
        tap_first * grad_conv
        + tap_second * extended[:, :, 1 : length + 1]
        + tap_third * extended[:, :, 2 : length + 2]
    )
    columns = w_in
    grad_input = lax.psum_scatter(
        jnp.einsum("icd,ict->dt", columns, grad_proj, precision=PRECISE),
        "ch",
        scatter_dimension=0,
        tiled=True,
    )
    return (output, grad_input, grad_filter)


def solution(mesh):
    in_specs = (
        P("ch", "seq"),
        P(None, "ch", None),
        P(None, None, "ch"),
        P("ch", "seq"),
        P("ch"),
        P("ch", None),
        P("ch", "seq"),
    )
    out_specs = (P("ch", "seq"), P("ch", "seq"), P("ch", "seq"))
    return jax.shard_map(body, mesh=mesh, in_specs=in_specs, out_specs=out_specs, check_vma=False)
```

profile of v0, /device:TPU:1, one launch (start us, length us, event | category | flops | bytes accessed | tf_op | source)
XLA Modules:
  0.0 433.5 jit_solution(6016858753336470031)
XLA Ops:
  7.2 9.9 %all_gather.6 = f32[256,512]{1,0:T(8,128)S(1)} all-gather(f32[64,512]{1,0:T(8,128)} %param.7), channel_id=1, replica_groups=mesh['seq'=64,'ch'=4] {'ch'}, dimensions={0}, use_global_device_ids=true | all-gather | bytes 655360 | tf_op jit(solution)/shard_map/all_gather | solution.py:132
  23.8 17.3 %all-to-all-start = ((f32[64,1,1024]{2,1,0:T(1,128)}), f32[64,1,1024]{2,1,0:T(1,128)S(1)}, u32[]{:S(2)}, u32[]{:S(2)}) async-start(f32[64,1,1024]{2,1,0:T(1,128)} %reshape.218), calls=%async_computation | async-start | bytes 524288 | tf_op jit(solution)/shard_map/all_to_all | solution.py:53
  41.3 13.2 %all-to-all-done = f32[64,1,1024]{2,1,0:T(1,128)S(1)} async-done(((f32[64,1,1024]{2,1,0:T(1,128)}), f32[64,1,1024]{2,1,0:T(1,128)S(1)}, u32[]{:S(2)}, u32[]{:S(2)}) %all-to-all-start) | async-done | bytes 262176 | tf_op jit(solution)/shard_map/all_to_all | solution.py:53
  59.8 24.5 %all_to_all.60 = f32[64,1,2048]{2,1,0:T(1,128)S(1)} all-to-all(f32[64,1,2048]{2,1,0:T(1,128)S(1)} %reshape.220), channel_id=1, replica_groups=mesh['seq'=64,'ch'=4] {'seq'}, dimensions={0} | all-to-all | bytes 1048576 | tf_op jit(solution)/shard_map/all_to_all | solution.py:73
  86.7 5.4 %fusion.19 = f32[2,64,512]{2,1,0:T(8,128)S(1)} fusion(f32[2,64,64,8]{1,3,0,2:T(8,128)S(1)} %get-tuple-element.26), kind=kOutput, calls=%fused_computation.40 | convolution fusion | flops 406323200 | bytes 524288 | tf_op jit(solution)/shard_map/ncj,jk->nck/dot_general | solution.py:78
  92.1 5.4 %fusion.17 = f32[2,64,512]{2,1,0:T(8,128)S(1)} fusion(f32[2,64,64,8]{1,3,0,2:T(8,128)S(1)} %get-tuple-element.27), kind=kOutput, calls=%fused_computation.38 | convolution fusion | flops 406323200 | bytes 524288 | tf_op jit(solution)/shard_map/ncj,jk->nck/dot_general | solution.py:81
  97.6 5.5 %convolution_add_fusion.1 = f32[2,64,512]{2,1,0:T(8,128)S(1)} fusion(f32[2,64,512]{2,1,0:T(8,128)S(1)} %fusion.19, f32[2,64,64,8]{1,3,0,2:T(8,128)S(1)} %get-tuple-element.27), kind=kOutput, calls=%fused_computation.16 | convolution fusion | flops 406388736 | bytes 786432 | tf_op jit(solution)/shard_map/ncj,jk->nck/dot_general | solution.py:78
  103.1 5.7 %convolution_subtract_fusion.3 = f32[2,64,512]{2,1,0:T(8,128)S(1)} fusion(f32[2,64,512]{2,1,0:T(8,128)S(1)} %fusion.17, f32[2,64,64,8]{1,3,0,2:T(8,128)S(1)} %get-tuple-element.26), kind=kOutput, calls=%fused_computation.15 | convolution fusion | flops 406388736 | bytes 786432 | tf_op jit(solution)/shard_map/ncj,jk->nck/dot_general | solution.py:81
  109.9 21.4 %all_to_all.61 = f32[64,1,2048]{2,1,0:T(1,128)S(1)} all-to-all(f32[64,1,2048]{2,1,0:T(1,128)S(1)} %reshape.222), channel_id=1, replica_groups=mesh['seq'=64,'ch'=4] {'seq'}, dimensions={0} | all-to-all | bytes 1048576 | tf_op jit(solution)/shard_map/all_to_all | solution.py:29
  134.9 7.1 %all-to-all-start.3 = ((f32[64,1,1024]{2,1,0:T(1,128)}), f32[64,1,1024]{2,1,0:T(1,128)S(1)}, u32[]{:S(2)}, u32[]{:S(2)}) async-start(f32[64,1,1024]{2,1,0:T(1,128)} %reshape.224), calls=%async_computation.3 | async-start | bytes 524288 | tf_op jit(solution)/shard_map/all_to_all | solution.py:41
  142.0 12.3 %all-to-all-done.3 = f32[64,1,1024]{2,1,0:T(1,128)S(1)} async-done(((f32[64,1,1024]{2,1,0:T(1,128)}), f32[64,1,1024]{2,1,0:T(1,128)S(1)}, u32[]{:S(2)}, u32[]{:S(2)}) %all-to-all-start.3) | async-done | bytes 262176 | tf_op jit(solution)/shard_map/all_to_all | solution.py:41
  155.7 4.8 %fusion.44 = f32[64,512]{1,0:T(8,128)S(1)} fusion(f32[2,64,64,8]{1,3,0,2:T(8,128)S(1)} %bitcast.257), kind=kOutput, calls=%fused_computation.68 | convolution fusion | flops 204996608 | bytes 393216 | tf_op jit(solution)/shard_map/nck,kj->ncj/dot_general | solution.py:98
  160.5 4.8 %fusion.46 = f32[64,512]{1,0:T(8,128)S(1)} fusion(f32[2,64,64,8]{1,3,0,2:T(8,128)S(1)} %bitcast.258), kind=kOutput, calls=%fused_computation.69 | convolution fusion | flops 204996608 | bytes 393216 | tf_op jit(solution)/shard_map/nck,kj->ncj/dot_general | solution.py:95
  165.4 4.8 %convolution_subtract_fusion.5 = f32[64,512]{1,0:T(8,128)S(1)} fusion(f32[64,512]{1,0:T(8,128)S(1)} %fusion.46, f32[2,64,64,8]{1,3,0,2:T(8,128)S(1)} %bitcast.259), kind=kOutput, calls=%fused_computation.24 | convolution fusion | flops 205029376 | bytes 524288 | tf_op jit(solution)/shard_map/nck,kj->ncj/dot_general | solution.py:95
  170.2 4.9 %multiply_subtract_fusion.6 = (f32[64,512]{1,0:T(8,128)S(1)}, f32[64,512]{1,0:T(8,128)S(1)}) fusion(f32[64,512]{1,0:T(8,128)S(1)} %convolution_subtract_fusion.5, f32[512]{0:T(512)S(1)} %get-tuple-element.47, f32[512]{0:T(512)S(1)} %get-tuple-element.48, f32[64,512]{1,0:T(8,128)S(1)} %fusion.44, f32[2,64,64,8]{1,3,0,2:T(8,128)S(1)} %bitcast.260), kind=kOutput, calls=%fused_computation.133 | convolution fusion | flops 205225984 | bytes 790528 | tf_op jit(solution)/shard_map/nck,kj->ncj/dot_general | solution.py:98
  182.9 10.5 %all-to-all-done.4 = f32[64,1,1024]{2,1,0:T(1,128)S(1)} async-done(((f32[64,1,1024]{2,1,0:T(1,128)}), f32[64,1,1024]{2,1,0:T(1,128)S(1)}, u32[]{:S(2)}, u32[]{:S(2)}) %all-to-all-start.4) | async-done | bytes 262176 | tf_op jit(solution)/shard_map/all_to_all | solution.py:112
  196.5 15.9 %all_to_all.62 = f32[64,1,512]{2,1,0:T(1,128)S(1)} all-to-all(f32[64,1,512]{2,1,0:T(1,128)S(1)} %reshape.228), channel_id=1, replica_groups=mesh['seq'=64,'ch'=4] {'seq'}, dimensions={0} | all-to-all | bytes 262144 | tf_op jit(solution)/shard_map/all_to_all | solution.py:119
  216.2 19.7 %all_to_all.63 = f32[64,1,512]{2,1,0:T(1,128)S(1)} all-to-all(f32[64,1,512]{2,1,0:T(1,128)S(1)} %reshape.230), channel_id=1, replica_groups=mesh['seq'=64,'ch'=4] {'seq'}, dimensions={0} | all-to-all | bytes 262144 | tf_op jit(solution)/shard_map/all_to_all | solution.py:53
  238.8 17.0 %all_to_all.64 = f32[64,1,1024]{2,1,0:T(1,128)S(1)} all-to-all(f32[64,1,1024]{2,1,0:T(1,128)S(1)} %reshape.232), channel_id=1, replica_groups=mesh['seq'=64,'ch'=4] {'seq'}, dimensions={0} | all-to-all | bytes 524288 | tf_op jit(solution)/shard_map/all_to_all | solution.py:73
  257.2 4.8 %fusion.48 = f32[64,512]{1,0:T(8,128)S(1)} fusion(f32[2,64,64,8]{1,3,0,2:T(8,128)S(1)} %bitcast.261), kind=kOutput, calls=%fused_computation.70 | convolution fusion | flops 204996608 | bytes 393216 | tf_op jit(solution)/shard_map/ncj,jk->nck/dot_general | solution.py:81
  266.8 4.8 %convolution_subtract_fusion.4 = f32[64,512]{1,0:T(8,128)S(1)} fusion(f32[64,512]{1,0:T(8,128)S(1)} %fusion.48, f32[2,64,64,8]{1,3,0,2:T(8,128)S(1)} %bitcast.263), kind=kOutput, calls=%fused_computation.21 | convolution fusion | flops 205029376 | bytes 524288 | tf_op jit(solution)/shard_map/ncj,jk->nck/dot_general | solution.py:81
  271.8 4.8 %convolution_add_fusion.2 = f32[64,512]{1,0:T(8,128)S(1)} fusion(f32[64,512]{1,0:T(8,128)S(1)} %fusion.42, f32[2,64,64,8]{1,3,0,2:T(8,128)S(1)} %bitcast.264), kind=kOutput, calls=%fused_computation.22 | convolution fusion | flops 205029376 | bytes 524288 | tf_op jit(solution)/shard_map/ncj,jk->nck/dot_general | solution.py:78
  277.1 16.9 %all_to_all.65 = f32[64,1,1024]{2,1,0:T(1,128)S(1)} all-to-all(f32[64,1,1024]{2,1,0:T(1,128)S(1)} %reshape.234), channel_id=1, replica_groups=mesh['seq'=64,'ch'=4] {'seq'}, dimensions={0} | all-to-all | bytes 524288 | tf_op jit(solution)/shard_map/all_to_all | solution.py:29
  296.4 19.1 %all_to_all.66 = f32[64,1,2048]{2,1,0:T(1,128)S(1)} all-to-all(f32[64,1,2048]{2,1,0:T(1,128)S(1)} %reshape.236), channel_id=1, replica_groups=mesh['seq'=64,'ch'=4] {'seq'}, dimensions={0} | all-to-all | bytes 1048576 | tf_op jit(solution)/shard_map/all_to_all | solution.py:41
  317.9 5.4 %fusion.13 = f32[2,64,512]{2,1,0:T(8,128)S(1)} fusion(f32[2,64,64,8]{1,3,0,2:T(8,128)S(1)} %get-tuple-element.22), kind=kOutput, calls=%fused_computation.34 | convolution fusion | flops 406323200 | bytes 524288 | tf_op jit(solution)/shard_map/nck,kj->ncj/dot_general | solution.py:98
  323.3 5.4 %fusion.15 = f32[2,64,512]{2,1,0:T(8,128)S(1)} fusion(f32[2,64,64,8]{1,3,0,2:T(8,128)S(1)} %get-tuple-element.23), kind=kOutput, calls=%fused_computation.36 | convolution fusion | flops 406323200 | bytes 524288 | tf_op jit(solution)/shard_map/nck,kj->ncj/dot_general | solution.py:95
  328.8 5.5 %convolution_subtract_fusion.1 = f32[2,64,512]{2,1,0:T(8,128)S(1)} fusion(f32[2,64,512]{2,1,0:T(8,128)S(1)} %fusion.15, f32[2,64,64,8]{1,3,0,2:T(8,128)S(1)} %get-tuple-element.22), kind=kOutput, calls=%fused_computation.11 | convolution fusion | flops 406388736 | bytes 786432 | tf_op jit(solution)/shard_map/nck,kj->ncj/dot_general | solution.py:95
  334.3 5.7 %multiply_subtract_fusion.1 = (f32[2,64,512]{2,1,0:T(8,128)S(1)}, f32[2,64,512]{2,1,0:T(8,128)S(1)}) fusion(f32[2,64,512]{2,1,0:T(8,128)S(1)} %convolution_subtract_fusion.1, f32[512]{0:T(512)S(1)} %get-tuple-element.47, f32[512]{0:T(512)S(1)} %get-tuple-element.48, f32[2,64,512]{2,1,0:T(8,128)S(1)} %fusion.13, f32[2,64,64,8]{1,3,0,2:T(8,128)S(1)} %get-tuple-element.23), kind=kOutput, calls=%fused_computation.109 | convolution fusion | flops 406781952 | bytes 1314816 | tf_op jit(solution)/shard_map/nck,kj->ncj/dot_general | solution.py:98
  341.1 19.7 %all_to_all.67 = f32[64,1,2048]{2,1,0:T(1,128)S(1)} all-to-all(f32[64,1,2048]{2,1,0:T(1,128)S(1)} %reshape.238), channel_id=1, replica_groups=mesh['seq'=64,'ch'=4] {'seq'}, dimensions={0} | all-to-all | bytes 1048576 | tf_op jit(solution)/shard_map/all_to_all | solution.py:112
  366.2 17.7 %all_to_all.68 = f32[64,1,1024]{2,1,0:T(1,128)S(1)} all-to-all(f32[64,1,1024]{2,1,0:T(1,128)S(1)} %reshape.240), channel_id=1, replica_groups=mesh['seq'=64,'ch'=4] {'seq'}, dimensions={0} | all-to-all | bytes 524288 | tf_op jit(solution)/shard_map/all_to_all | solution.py:119
  395.2 17.1 %all_gather.7 = f32[256,512]{1,0:T(8,128)S(1)} all-gather(f32[64,512]{1,0:T(8,128)S(1)} %get-tuple-element.39), channel_id=1, replica_groups=mesh['seq'=64,'ch'=4] {'ch'}, dimensions={0}, use_global_device_ids=true | all-gather | bytes 655360 | tf_op jit(solution)/shard_map/all_gather | solution.py:155
  413.4 13.1 %reduce-scatter.7.cloned.1.call-done = f32[64,512]{1,0:T(8,128)} async-done(((f32[256,512]{1,0:T(8,128)}), f32[64,512]{1,0:T(8,128)}) %reduce-scatter.7.cloned.1.call-update) | async-done | bytes 131088
  (130 shorter events, 68.1 us)
Async XLA Ops:
  7.2 9.9 %copy-start = (f32[3,64,256]{2,1,0:T(8,128)S(1)}, f32[3,64,256]{2,1,0:T(8,128)}, u32[]{:S(2)}) copy-start(f32[3,64,256]{2,1,0:T(8,128)} %param.8) | copy-start | bytes 589828
  17.6 2.6 copy-start.3
  17.7 4.5 %collective-permute-start = (f32[3,64,2]{2,1,0:T(8,128)S(1)}, f32[3,64,2]{2,1,0:T(8,128)S(1)}, u32[]{:S(2)}, u32[]{:S(2)}) collective-permute-start(f32[3,64,2]{2,1,0:T(8,128)S(1)} %slice.167), channel_id=1, source_target_pairs={{0,4},{4,8},{8,12},{12,16},{16,20},{20,24},{24,28},{28,32},{32,36}... | collective-permute-start | bytes 4616 | tf_op jit(solution)/shard_map/ppermute | solution.py:13
  20.3 0.7 copy-start.5
  23.8 30.6 %all-to-all-start = ((f32[64,1,1024]{2,1,0:T(1,128)}), f32[64,1,1024]{2,1,0:T(1,128)S(1)}, u32[]{:S(2)}, u32[]{:S(2)}) async-start(f32[64,1,1024]{2,1,0:T(1,128)} %reshape.218), calls=%async_computation | async-start | bytes 524288 | tf_op jit(solution)/shard_map/all_to_all | solution.py:53
  134.9 19.4 %all-to-all-start.3 = ((f32[64,1,1024]{2,1,0:T(1,128)}), f32[64,1,1024]{2,1,0:T(1,128)S(1)}, u32[]{:S(2)}, u32[]{:S(2)}) async-start(f32[64,1,1024]{2,1,0:T(1,128)} %reshape.224), calls=%async_computation.3 | async-start | bytes 524288 | tf_op jit(solution)/shard_map/all_to_all | solution.py:41
  176.4 5.0 %copy-start.2 = (f32[64,256]{1,0:T(8,128)S(1)}, f32[64,256]{1,0:T(8,128)}, u32[]{:S(2)}) copy-start(f32[64,256]{1,0:T(8,128)} %param.12) | copy-start | bytes 196612
  176.4 5.0 %copy-start.4 = (f32[64,512]{1,0:T(8,128)S(1)}, f32[64,512]{1,0:T(8,128)}, u32[]{:S(2)}) copy-start(f32[64,512]{1,0:T(8,128)} %param.13) | copy-start | bytes 393220
  176.4 17.0 %all-to-all-start.4 = ((f32[64,1,1024]{2,1,0:T(1,128)}), f32[64,1,1024]{2,1,0:T(1,128)S(1)}, u32[]{:S(2)}, u32[]{:S(2)}) async-start(f32[64,1,1024]{2,1,0:T(1,128)} %reshape.226), calls=%async_computation.4 | async-start | bytes 524288 | tf_op jit(solution)/shard_map/all_to_all | solution.py:112
  181.2 32.5 %reduce-scatter.5.cloned.1.call-start = ((), (), s32[]{:S(2)}) async-start(), calls=%async_computation.14 | async-start | bytes 655360 | tf_op jit(solution)/shard_map/reduce_scatter | solution.py:157
  182.8 243.7 %reduce-scatter.7.cloned.1.call-start = ((), (), s32[]{:S(2)}) async-start(), calls=%async_computation.15 | async-start | bytes 655360
  213.5 0.7 copy-start.6
  385.3 0.9 copy-start.1
  386.4 5.7 %collective-permute-start.1 = (f32[3,64,2]{2,1,0:T(8,128)S(1)}, f32[3,64,2]{2,1,0:T(8,128)S(1)}, u32[]{:S(2)}, u32[]{:S(2)}) collective-permute-start(f32[3,64,2]{2,1,0:T(8,128)S(1)} %slice.192), channel_id=1, source_target_pairs={{4,0},{8,4},{12,8},{16,12},{20,16},{24,20},{28,24},{32,28},{36,32}... | collective-permute-start | bytes 4616 | tf_op jit(solution)/shard_map/ppermute | solution.py:13
Sparse Core Ops, SparseCore 0:
  184.5 26.0 reduce-scatter.4
  394.5 31.9 reduce-scatter.6
where the time goes:
time: 440 us; the launch traced here: 434 us
  blocking collectives  199 us (45%)
  matrix products  92.8 us (21%)
  waiting for transfers between devices  54.6 us (12%)
  starting transfers between devices  33.2 us (8%)
  other arithmetic  20.1 us (5%)
  local copies, waits for them, and re-layouts  18.8 us (4%)
  between operations  15.1 us (3%)
    all_to_all x2, blocking collectives, to_spectrum(): lax.all_to_all(stacked, 'seq', split_axis=2, concat_axis=2, tiled=True)  41.5 us
    all_to_all x2, blocking collectives, to_sorted(): lax.all_to_all(stacked, 'seq', split_axis=2, concat_axis=2, tiled=True)  38.4 us
    all_to_all x2, blocking collectives, from_spectrum(): lax.all_to_all(pieces, 'seq', split_axis=2, concat_axis=2, tiled=True)  33.6 us
    all_to_all x1, blocking collectives, from_spectrum(): lax.all_to_all(stacked, 'seq', split_axis=2, concat_axis=2, tiled=True)  19.7 us
    all_to_all x1, blocking collectives, to_spectrum(): lax.all_to_all(signal.reshape(rows_in, channels, shards, slab_len), 'seq'...  19.7 us
    all_to_all x1, blocking collectives, from_sorted(): lax.all_to_all(stacked, 'seq', split_axis=2, concat_axis=2, tiled=True)  19.1 us
    all_to_all x1, starting transfers between devices, to_spectrum(): lax.all_to_all(signal.reshape(rows_in, channels, shards, slab_len), 'seq'...  17.3 us
    all_gather x1, blocking collectives, body(): lax.all_gather(out_gate, 'ch', axis=0, tiled=True)  17.1 us
  transfers between devices with their start and end apart: 7, of which 6 were waited for; matrix products, arithmetic and copies ran while one was open for 2% of the time, Pallas kernels for 0%

commit v1 on v0

--- a/solution.py
+++ b/solution.py
@@ -152,7 +152,13 @@
     mixed = convolution + skip[:, None] * gated
     out_gate = convolved[0] * mixed
     columns = w_out
-    output = jnp.dot(columns, lax.all_gather(out_gate, "ch", axis=0, tiled=True), precision=PRECISE)
+    output = jnp.dot(
+        columns,
+        jnp.concatenate(
+            lax.all_to_all(jnp.stack([out_gate] * lax.axis_size("ch")), "ch", 0, 0), axis=0
+        ),
+        precision=PRECISE,
+    )
     columns = w_out
     grad_gate = lax.psum_scatter(
         jnp.dot(columns.T, cotangent, precision=PRECISE), "ch", scatter_dimension=0, tiled=True

time: 440 us -> 439 us (level)
    all_to_all x0 -> x1, blocking collectives: none -> 21 us  [body(): lax.all_to_all(jnp.stack([out_gate] * lax.axis_size('ch')), 'ch', 0, 0)]
    all_gather x1 -> x0, blocking collectives: 17.1 us -> none  [body(): lax.all_gather(out_gate, 'ch', axis=0, tiled=True)]
    unnamed x46 -> x52, local copies, waits for them, and re-layouts: 14.1 us -> 13.3 us
where the time goes in v1:
time: 439 us; the launch traced here: 432 us
  blocking collectives  203 us (46%)
  matrix products  92.7 us (21%)
  waiting for transfers between devices  50.5 us (12%)
  starting transfers between devices  33.2 us (8%)
  other arithmetic  19.5 us (4%)
  local copies, waits for them, and re-layouts  18.2 us (4%)
  between operations  15.2 us (3%)
    all_to_all x2, blocking collectives, to_spectrum(): lax.all_to_all(stacked, 'seq', split_axis=2, concat_axis=2, tiled=True)  41.5 us
    all_to_all x2, blocking collectives, to_sorted(): lax.all_to_all(stacked, 'seq', split_axis=2, concat_axis=2, tiled=True)  38.4 us
    all_to_all x2, blocking collectives, from_spectrum(): lax.all_to_all(pieces, 'seq', split_axis=2, concat_axis=2, tiled=True)  33.3 us
    all_to_all x1, blocking collectives, body(): lax.all_to_all(jnp.stack([out_gate] * lax.axis_size('ch')), 'ch', 0, 0)  21 us
    all_to_all x1, blocking collectives, from_spectrum(): lax.all_to_all(stacked, 'seq', split_axis=2, concat_axis=2, tiled=True)  19.9 us
    all_to_all x1, blocking collectives, to_spectrum(): lax.all_to_all(signal.reshape(rows_in, channels, shards, slab_len), 'seq'...  19.7 us
    all_to_all x1, blocking collectives, from_sorted(): lax.all_to_all(stacked, 'seq', split_axis=2, concat_axis=2, tiled=True)  19.1 us
    all_to_all x1, starting transfers between devices, to_spectrum(): lax.all_to_all(signal.reshape(rows_in, channels, shards, slab_len), 'seq'...  17.3 us
  transfers between devices with their start and end apart: 7, of which 6 were waited for; matrix products, arithmetic and copies ran while one was open for 2% of the time, Pallas kernels for 0%

profile of v1, /device:TPU:1, one launch (start us, length us, event | category | flops | bytes accessed | tf_op | source)
XLA Modules:
  0.0 432.1 jit_solution(10710695608534171154)
XLA Ops:
  7.2 9.9 %all_gather.3 = f32[256,512]{1,0:T(8,128)S(1)} all-gather(f32[64,512]{1,0:T(8,128)} %param.7), channel_id=1, replica_groups=mesh['seq'=64,'ch'=4] {'ch'}, dimensions={0}, use_global_device_ids=true | all-gather | bytes 655360 | tf_op jit(solution)/shard_map/all_gather | solution.py:132
  23.8 17.3 %all-to-all-start = ((f32[64,1,1024]{2,1,0:T(1,128)}), f32[64,1,1024]{2,1,0:T(1,128)S(1)}, u32[]{:S(2)}, u32[]{:S(2)}) async-start(f32[64,1,1024]{2,1,0:T(1,128)} %reshape.229), calls=%async_computation | async-start | bytes 524288 | tf_op jit(solution)/shard_map/all_to_all | solution.py:53
  41.3 13.2 %all-to-all-done = f32[64,1,1024]{2,1,0:T(1,128)S(1)} async-done(((f32[64,1,1024]{2,1,0:T(1,128)}), f32[64,1,1024]{2,1,0:T(1,128)S(1)}, u32[]{:S(2)}, u32[]{:S(2)}) %all-to-all-start) | async-done | bytes 262176 | tf_op jit(solution)/shard_map/all_to_all | solution.py:53
  59.8 24.5 %all_to_all.65 = f32[64,1,2048]{2,1,0:T(1,128)S(1)} all-to-all(f32[64,1,2048]{2,1,0:T(1,128)S(1)} %reshape.231), channel_id=1, replica_groups=mesh['seq'=64,'ch'=4] {'seq'}, dimensions={0} | all-to-all | bytes 1048576 | tf_op jit(solution)/shard_map/all_to_all | solution.py:73
  86.7 5.4 %fusion.19 = f32[2,64,512]{2,1,0:T(8,128)S(1)} fusion(f32[2,64,64,8]{1,3,0,2:T(8,128)S(1)} %get-tuple-element.24), kind=kOutput, calls=%fused_computation.40 | convolution fusion | flops 406323200 | bytes 524288 | tf_op jit(solution)/shard_map/ncj,jk->nck/dot_general | solution.py:78
  92.1 5.4 %fusion.17 = f32[2,64,512]{2,1,0:T(8,128)S(1)} fusion(f32[2,64,64,8]{1,3,0,2:T(8,128)S(1)} %get-tuple-element.25), kind=kOutput, calls=%fused_computation.38 | convolution fusion | flops 406323200 | bytes 524288 | tf_op jit(solution)/shard_map/ncj,jk->nck/dot_general | solution.py:81
  97.6 5.5 %convolution_add_fusion.1 = f32[2,64,512]{2,1,0:T(8,128)S(1)} fusion(f32[2,64,512]{2,1,0:T(8,128)S(1)} %fusion.19, f32[2,64,64,8]{1,3,0,2:T(8,128)S(1)} %get-tuple-element.25), kind=kOutput, calls=%fused_computation.16 | convolution fusion | flops 406388736 | bytes 786432 | tf_op jit(solution)/shard_map/ncj,jk->nck/dot_general | solution.py:78
  103.0 5.7 %convolution_subtract_fusion.3 = f32[2,64,512]{2,1,0:T(8,128)S(1)} fusion(f32[2,64,512]{2,1,0:T(8,128)S(1)} %fusion.17, f32[2,64,64,8]{1,3,0,2:T(8,128)S(1)} %get-tuple-element.24), kind=kOutput, calls=%fused_computation.15 | convolution fusion | flops 406388736 | bytes 786432 | tf_op jit(solution)/shard_map/ncj,jk->nck/dot_general | solution.py:81
  109.9 21.4 %all_to_all.66 = f32[64,1,2048]{2,1,0:T(1,128)S(1)} all-to-all(f32[64,1,2048]{2,1,0:T(1,128)S(1)} %reshape.233), channel_id=1, replica_groups=mesh['seq'=64,'ch'=4] {'seq'}, dimensions={0} | all-to-all | bytes 1048576 | tf_op jit(solution)/shard_map/all_to_all | solution.py:29
  134.9 7.1 %all-to-all-start.3 = ((f32[64,1,1024]{2,1,0:T(1,128)}), f32[64,1,1024]{2,1,0:T(1,128)S(1)}, u32[]{:S(2)}, u32[]{:S(2)}) async-start(f32[64,1,1024]{2,1,0:T(1,128)} %reshape.235), calls=%async_computation.3 | async-start | bytes 524288 | tf_op jit(solution)/shard_map/all_to_all | solution.py:41
  142.0 12.3 %all-to-all-done.3 = f32[64,1,1024]{2,1,0:T(1,128)S(1)} async-done(((f32[64,1,1024]{2,1,0:T(1,128)}), f32[64,1,1024]{2,1,0:T(1,128)S(1)}, u32[]{:S(2)}, u32[]{:S(2)}) %all-to-all-start.3) | async-done | bytes 262176 | tf_op jit(solution)/shard_map/all_to_all | solution.py:41
  155.7 4.8 %fusion.44 = f32[64,512]{1,0:T(8,128)S(1)} fusion(f32[2,64,64,8]{1,3,0,2:T(8,128)S(1)} %bitcast.262), kind=kOutput, calls=%fused_computation.68 | convolution fusion | flops 204996608 | bytes 393216 | tf_op jit(solution)/shard_map/nck,kj->ncj/dot_general | solution.py:98
  160.5 4.8 %fusion.46 = f32[64,512]{1,0:T(8,128)S(1)} fusion(f32[2,64,64,8]{1,3,0,2:T(8,128)S(1)} %bitcast.263), kind=kOutput, calls=%fused_computation.69 | convolution fusion | flops 204996608 | bytes 393216 | tf_op jit(solution)/shard_map/nck,kj->ncj/dot_general | solution.py:95
  165.3 4.8 %convolution_subtract_fusion.5 = f32[64,512]{1,0:T(8,128)S(1)} fusion(f32[64,512]{1,0:T(8,128)S(1)} %fusion.46, f32[2,64,64,8]{1,3,0,2:T(8,128)S(1)} %bitcast.264), kind=kOutput, calls=%fused_computation.24 | convolution fusion | flops 205029376 | bytes 524288 | tf_op jit(solution)/shard_map/nck,kj->ncj/dot_general | solution.py:95
  170.2 4.9 %multiply_subtract_fusion.6 = (f32[64,512]{1,0:T(8,128)S(1)}, f32[64,512]{1,0:T(8,128)S(1)}) fusion(f32[64,512]{1,0:T(8,128)S(1)} %convolution_subtract_fusion.5, f32[512]{0:T(512)S(1)} %get-tuple-element.45, f32[512]{0:T(512)S(1)} %get-tuple-element.46, f32[64,512]{1,0:T(8,128)S(1)} %fusion.44, f32[2,64,64,8]{1,3,0,2:T(8,128)S(1)} %bitcast.265), kind=kOutput, calls=%fused_computation.135 | convolution fusion | flops 205225984 | bytes 790528 | tf_op jit(solution)/shard_map/nck,kj->ncj/dot_general | solution.py:98
  182.9 10.5 %all-to-all-done.4 = f32[64,1,1024]{2,1,0:T(1,128)S(1)} async-done(((f32[64,1,1024]{2,1,0:T(1,128)}), f32[64,1,1024]{2,1,0:T(1,128)S(1)}, u32[]{:S(2)}, u32[]{:S(2)}) %all-to-all-start.4) | async-done | bytes 262176 | tf_op jit(solution)/shard_map/all_to_all | solution.py:112
  196.5 15.9 %all_to_all.67 = f32[64,1,512]{2,1,0:T(1,128)S(1)} all-to-all(f32[64,1,512]{2,1,0:T(1,128)S(1)} %reshape.239), channel_id=1, replica_groups=mesh['seq'=64,'ch'=4] {'seq'}, dimensions={0} | all-to-all | bytes 262144 | tf_op jit(solution)/shard_map/all_to_all | solution.py:119
  215.5 19.7 %all_to_all.68 = f32[64,1,512]{2,1,0:T(1,128)S(1)} all-to-all(f32[64,1,512]{2,1,0:T(1,128)S(1)} %reshape.241), channel_id=1, replica_groups=mesh['seq'=64,'ch'=4] {'seq'}, dimensions={0} | all-to-all | bytes 262144 | tf_op jit(solution)/shard_map/all_to_all | solution.py:53
  238.1 17.0 %all_to_all.69 = f32[64,1,1024]{2,1,0:T(1,128)S(1)} all-to-all(f32[64,1,1024]{2,1,0:T(1,128)S(1)} %reshape.243), channel_id=1, replica_groups=mesh['seq'=64,'ch'=4] {'seq'}, dimensions={0} | all-to-all | bytes 524288 | tf_op jit(solution)/shard_map/all_to_all | solution.py:73
  256.5 4.8 %fusion.48 = f32[64,512]{1,0:T(8,128)S(1)} fusion(f32[2,64,64,8]{1,3,0,2:T(8,128)S(1)} %bitcast.266), kind=kOutput, calls=%fused_computation.70 | convolution fusion | flops 204996608 | bytes 393216 | tf_op jit(solution)/shard_map/ncj,jk->nck/dot_general | solution.py:81
  266.2 4.8 %convolution_subtract_fusion.4 = f32[64,512]{1,0:T(8,128)S(1)} fusion(f32[64,512]{1,0:T(8,128)S(1)} %fusion.48, f32[2,64,64,8]{1,3,0,2:T(8,128)S(1)} %bitcast.268), kind=kOutput, calls=%fused_computation.21 | convolution fusion | flops 205029376 | bytes 524288 | tf_op jit(solution)/shard_map/ncj,jk->nck/dot_general | solution.py:81
  271.1 4.8 %convolution_add_fusion.2 = f32[64,512]{1,0:T(8,128)S(1)} fusion(f32[64,512]{1,0:T(8,128)S(1)} %fusion.42, f32[2,64,64,8]{1,3,0,2:T(8,128)S(1)} %bitcast.269), kind=kOutput, calls=%fused_computation.22 | convolution fusion | flops 205029376 | bytes 524288 | tf_op jit(solution)/shard_map/ncj,jk->nck/dot_general | solution.py:78
  276.5 16.9 %all_to_all.70 = f32[64,1,1024]{2,1,0:T(1,128)S(1)} all-to-all(f32[64,1,1024]{2,1,0:T(1,128)S(1)} %reshape.245), channel_id=1, replica_groups=mesh['seq'=64,'ch'=4] {'seq'}, dimensions={0} | all-to-all | bytes 524288 | tf_op jit(solution)/shard_map/all_to_all | solution.py:29
  295.7 19.1 %all_to_all.71 = f32[64,1,2048]{2,1,0:T(1,128)S(1)} all-to-all(f32[64,1,2048]{2,1,0:T(1,128)S(1)} %reshape.247), channel_id=1, replica_groups=mesh['seq'=64,'ch'=4] {'seq'}, dimensions={0} | all-to-all | bytes 1048576 | tf_op jit(solution)/shard_map/all_to_all | solution.py:41
  317.2 5.4 %fusion.13 = f32[2,64,512]{2,1,0:T(8,128)S(1)} fusion(f32[2,64,64,8]{1,3,0,2:T(8,128)S(1)} %get-tuple-element.20), kind=kOutput, calls=%fused_computation.34 | convolution fusion | flops 406323200 | bytes 524288 | tf_op jit(solution)/shard_map/nck,kj->ncj/dot_general | solution.py:98
  322.7 5.4 %fusion.15 = f32[2,64,512]{2,1,0:T(8,128)S(1)} fusion(f32[2,64,64,8]{1,3,0,2:T(8,128)S(1)} %get-tuple-element.21), kind=kOutput, calls=%fused_computation.36 | convolution fusion | flops 406323200 | bytes 524288 | tf_op jit(solution)/shard_map/nck,kj->ncj/dot_general | solution.py:95
  328.1 5.5 %convolution_subtract_fusion.1 = f32[2,64,512]{2,1,0:T(8,128)S(1)} fusion(f32[2,64,512]{2,1,0:T(8,128)S(1)} %fusion.15, f32[2,64,64,8]{1,3,0,2:T(8,128)S(1)} %get-tuple-element.20), kind=kOutput, calls=%fused_computation.11 | convolution fusion | flops 406388736 | bytes 786432 | tf_op jit(solution)/shard_map/nck,kj->ncj/dot_general | solution.py:95
  333.6 5.7 %multiply_subtract_fusion.1 = (f32[2,64,512]{2,1,0:T(8,128)S(1)}, f32[2,64,512]{2,1,0:T(8,128)S(1)}) fusion(f32[2,64,512]{2,1,0:T(8,128)S(1)} %convolution_subtract_fusion.1, f32[512]{0:T(512)S(1)} %copy-done.7, f32[512]{0:T(512)S(1)} %copy-done.9, f32[2,64,512]{2,1,0:T(8,128)S(1)} %fusion.13, f32[2,64,64,8]{1,3,0,2:T(8,128)S(1)} %get-tuple-element.21), kind=kOutput, calls=%fused_computation.109 | convolution fusion | flops 406781952 | bytes 1314816 | tf_op jit(solution)/shard_map/nck,kj->ncj/dot_general | solution.py:98
  340.5 19.9 %all_to_all.72 = f32[64,1,2048]{2,1,0:T(1,128)S(1)} all-to-all(f32[64,1,2048]{2,1,0:T(1,128)S(1)} %reshape.249), channel_id=1, replica_groups=mesh['seq'=64,'ch'=4] {'seq'}, dimensions={0} | all-to-all | bytes 1048576 | tf_op jit(solution)/shard_map/all_to_all | solution.py:112
  365.7 17.4 %all_to_all.73 = f32[64,1,1024]{2,1,0:T(1,128)S(1)} all-to-all(f32[64,1,1024]{2,1,0:T(1,128)S(1)} %reshape.251), channel_id=1, replica_groups=mesh['seq'=64,'ch'=4] {'seq'}, dimensions={0} | all-to-all | bytes 524288 | tf_op jit(solution)/shard_map/all_to_all | solution.py:119
  393.1 21.0 %all_to_all.74 = f32[4,64,512]{2,1,0:T(8,128)S(1)} all-to-all(f32[4,64,512]{2,1,0:T(8,128)S(1)} %stack.38), channel_id=1, replica_groups=mesh['seq'=64,'ch'=4] {'ch'}, dimensions={0} | all-to-all | bytes 1048576 | tf_op jit(solution)/shard_map/all_to_all | solution.py:158
  416.0 9.1 %reduce-scatter.7.cloned.1.call-done = f32[64,512]{1,0:T(8,128)} async-done(((f32[256,512]{1,0:T(8,128)}), f32[64,512]{1,0:T(8,128)}) %reduce-scatter.7.cloned.1.call-update) | async-done | bytes 131088
  (140 shorter events, 66.7 us)
Async XLA Ops:
  7.2 9.9 %copy-start = (f32[3,64,256]{2,1,0:T(8,128)S(1)}, f32[3,64,256]{2,1,0:T(8,128)}, u32[]{:S(2)}) copy-start(f32[3,64,256]{2,1,0:T(8,128)} %param.8) | copy-start | bytes 589828
  17.6 2.6 copy-start.2
  17.7 4.5 %collective-permute-start = (f32[3,64,2]{2,1,0:T(8,128)S(1)}, f32[3,64,2]{2,1,0:T(8,128)S(1)}, u32[]{:S(2)}, u32[]{:S(2)}) collective-permute-start(f32[3,64,2]{2,1,0:T(8,128)S(1)} %slice.167), channel_id=1, source_target_pairs={{0,4},{4,8},{8,12},{12,16},{16,20},{20,24},{24,28},{28,32},{32,36}... | collective-permute-start | bytes 4616 | tf_op jit(solution)/shard_map/ppermute | solution.py:13
  20.3 0.7 copy-start.4
  23.8 30.6 %all-to-all-start = ((f32[64,1,1024]{2,1,0:T(1,128)}), f32[64,1,1024]{2,1,0:T(1,128)S(1)}, u32[]{:S(2)}, u32[]{:S(2)}) async-start(f32[64,1,1024]{2,1,0:T(1,128)} %reshape.229), calls=%async_computation | async-start | bytes 524288 | tf_op jit(solution)/shard_map/all_to_all | solution.py:53
  134.9 19.4 %all-to-all-start.3 = ((f32[64,1,1024]{2,1,0:T(1,128)}), f32[64,1,1024]{2,1,0:T(1,128)S(1)}, u32[]{:S(2)}, u32[]{:S(2)}) async-start(f32[64,1,1024]{2,1,0:T(1,128)} %reshape.235), calls=%async_computation.3 | async-start | bytes 524288 | tf_op jit(solution)/shard_map/all_to_all | solution.py:41
  142.0 28.2 %copy-start.6 = (f32[512]{0:T(512)}, f32[512]{0:T(512)S(1)}, u32[]{:S(2)}) copy-start(f32[512]{0:T(512)S(1)} %get-tuple-element.45) | copy-start | bytes 6148
  142.0 28.2 %copy-start.8 = (f32[512]{0:T(512)}, f32[512]{0:T(512)S(1)}, u32[]{:S(2)}) copy-start(f32[512]{0:T(512)S(1)} %get-tuple-element.46) | copy-start | bytes 6148
  176.4 5.0 %copy-start.1 = (f32[64,256]{1,0:T(8,128)S(1)}, f32[64,256]{1,0:T(8,128)}, u32[]{:S(2)}) copy-start(f32[64,256]{1,0:T(8,128)} %param.12) | copy-start | bytes 196612
  176.4 5.0 %copy-start.3 = (f32[64,512]{1,0:T(8,128)S(1)}, f32[64,512]{1,0:T(8,128)}, u32[]{:S(2)}) copy-start(f32[64,512]{1,0:T(8,128)} %param.13) | copy-start | bytes 393220
  176.4 17.0 %all-to-all-start.4 = ((f32[64,1,1024]{2,1,0:T(1,128)}), f32[64,1,1024]{2,1,0:T(1,128)S(1)}, u32[]{:S(2)}, u32[]{:S(2)}) async-start(f32[64,1,1024]{2,1,0:T(1,128)} %reshape.237), calls=%async_computation.4 | async-start | bytes 524288 | tf_op jit(solution)/shard_map/all_to_all | solution.py:112
  181.2 32.5 %reduce-scatter.5.cloned.1.call-start = ((), (), s32[]{:S(2)}) async-start(), calls=%async_computation.15 | async-start | bytes 655360 | tf_op jit(solution)/shard_map/reduce_scatter | solution.py:163
  182.8 242.2 %reduce-scatter.7.cloned.1.call-start = ((), (), s32[]{:S(2)}) async-start(), calls=%async_computation.16 | async-start | bytes 655360
  213.5 0.7 copy-start.5
  328.1 5.5 %copy-start.7 = (f32[512]{0:T(512)S(1)}, f32[512]{0:T(512)}, u32[]{:S(2)}) copy-start(f32[512]{0:T(512)} %copy-done.6) | copy-start | bytes 6148
  328.1 5.5 %copy-start.9 = (f32[512]{0:T(512)S(1)}, f32[512]{0:T(512)}, u32[]{:S(2)}) copy-start(f32[512]{0:T(512)} %copy-done.8) | copy-start | bytes 6148
  384.9 5.7 %collective-permute-start.1 = (f32[3,64,2]{2,1,0:T(8,128)S(1)}, f32[3,64,2]{2,1,0:T(8,128)S(1)}, u32[]{:S(2)}, u32[]{:S(2)}) collective-permute-start(f32[3,64,2]{2,1,0:T(8,128)S(1)} %slice.192), channel_id=1, source_target_pairs={{4,0},{8,4},{12,8},{16,12},{20,16},{24,20},{28,24},{32,28},{36,32}... | collective-permute-start | bytes 4616 | tf_op jit(solution)/shard_map/ppermute | solution.py:13
Sparse Core Ops, SparseCore 0:
  184.5 26.0 reduce-scatter.4
  393.0 32.0 reduce-scatter.6
